TPU v7x, 256 devices: a whole 4x4x8 slice. The times are simulated.
256 devices in a mesh: row: 16 (over y, x), col: 8 (over z), chan: 2 (over core).
Axes of the slice: x: 4, y: 4, z: 8, core: 2. Of those that a mesh axis runs over, the one named last changes fastest.
Arguments:
- samples: bfloat16 [8192, 2, 8192], P(('chan', 'col'), None, 'row'), parts along dimension 0, may hold values from -6 to 6
- sky_model: bfloat16 [8192, 2, 4096], P(('chan', 'row'), None, 'col'), parts along dimension 0, may hold values from -128 to 128, as said below
- initial_gains: float32 [2, 8192], P(None, ('chan', 'row', 'col')), parts along dimension 1, may hold values from -3 to 3, as said below
Outputs:
- calibrated: float32 [2, 8192], P(None, ('chan', 'row', 'col')), parts along dimension 1
There are 2 independent parts, one for each index of `chan`. A program takes and returns all parts, laid end to end along the dimension named above; each array names one. Nothing has to cross between parts.
Inputs may be any that keep to these rules, and one draw needn't show every extreme that they name: sky_model is Hermitian: sky_model[q,0,p] = sky_model[p,0,q] and sky_model[q,1,p] = -sky_model[p,1,q]. `initial_gains`: every initial gain has magnitude between 0.3 and 3.
All inputs are finite; a program needn't handle non-finite values.
Results may differ from a plain program's by a relative error of at most 0.0003.
Values may be sent and summed in bfloat16 or wider, within the bound.
No kernel may reach another device: no remote copies, remote signals or barrier semaphores. Data moves between devices by JAX's collectives and lax.ppermute only.
A program may use at most 192 MiB of HBM per device.

v0:
```python
import jax
import jax.numpy as jnp
from jax import lax
from jax.sharding import PartitionSpec as P

ITERS = 3


def body(samples, sky_model, initial_gains):
    row_count = lax.axis_size("row")
    column_count = lax.axis_size("col")
    row_index = lax.axis_index("row")
    column_index = lax.axis_index("col")
    block_column = samples.shape[0]
    block_row = sky_model.shape[0]
    share_size = initial_gains.shape[1]
    contract_last = (((1,), (1,)), ((), ()))
    upper_limit = lax.Precision.HIGHEST
    own_start = (row_index * column_count + column_index) * share_size
    flattened = samples.reshape(block_column, -1)
    rotated = jnp.concatenate([-samples[:, 1, :], samples[:, 0, :]], axis=1)
    right_side = jnp.concatenate([flattened, rotated], axis=0)
    all_antennas = lax.all_gather(flattened, "col", axis=0, tiled=True)
    vis_tile = lax.psum_scatter(
        lax.dot_general(
            all_antennas, right_side, contract_last, preferred_element_type=jnp.float32
        ),
        "row",
        scatter_dimension=0,
        tiled=True,
    )
    vis_real = vis_tile[:, :block_column]
    vis_imag = vis_tile[:, block_column:]
    model_real = sky_model[:, 0, :].astype(jnp.float32)
    model_imag = sky_model[:, 1, :].astype(jnp.float32)
    global_rows = row_index * block_row + lax.broadcasted_iota(
        jnp.int32, (block_row, block_column), 0
    )
    global_columns = column_index * block_column + lax.broadcasted_iota(
        jnp.int32, (block_row, block_column), 1
    )
    cross_mask = (global_rows != global_columns).astype(jnp.float32)
    weight_real = (vis_real * model_real + vis_imag * model_imag) * cross_mask
    weight_imag = (vis_real * model_imag - vis_imag * model_real) * cross_mask
    model_power = (model_real * model_real + model_imag * model_imag) * cross_mask
    stacked = jnp.concatenate([weight_real, weight_imag], axis=0)
    row_gains = lax.all_gather(initial_gains, "col", axis=1, tiled=True)
    everything = row_gains
    for iteration in range(ITERS):
        gain_real = row_gains[0]
        gain_imag = row_gains[1]
        left_rows = jnp.stack(
            [jnp.concatenate([gain_real, -gain_imag]), jnp.concatenate([gain_imag, gain_real])]
        )
        totals = jnp.dot(left_rows, stacked, precision=upper_limit)
        energy = jnp.dot(
            gain_real * gain_real + gain_imag * gain_imag, model_power, precision=upper_limit
        )
        totals, energy = (totals, energy)
        totals, energy = (
            lax.psum_scatter(totals, "row", scatter_dimension=1, tiled=True),
            lax.psum_scatter(energy, "row", scatter_dimension=0, tiled=True),
        )
        updated = totals / energy[None, :]
        if iteration == 1:
            previous = lax.dynamic_slice_in_dim(
                everything, (column_index * row_count + row_index) * share_size, share_size, 1
            )
            updated = 0.5 * (updated + previous)
        gain_block = lax.all_gather(updated, "row", axis=1, tiled=True)
        everything = lax.all_gather(gain_block, "col", axis=1, tiled=True)
        row_gains = lax.dynamic_slice_in_dim(everything, row_index * block_row, block_row, 1)
    return lax.dynamic_slice_in_dim(everything, own_start, share_size, 1)


def solution(mesh):
    return jax.shard_map(
        body,
        mesh=mesh,
        in_specs=(
            P(("chan", "col"), None, "row"),
            P(("chan", "row"), None, "col"),
            P(None, ("chan", "row", "col")),
        ),
        out_specs=P(None, ("chan", "row", "col")),
        check_vma=False,
    )
```

profile of v0, /device:TPU:64, one launch (start us, length us, event | category | flops | bytes accessed | tf_op | source)
XLA Modules:
  0.0 626.5 jit_solution(196961169140078920)
XLA Ops:
  6.5 0.0 copy-start
  6.5 0.0 all-gather.6.cloned.1.call-start
  6.5 2.5 copy.41
  9.1 0.0 copy-start.1
  9.1 0.0 all-gather.6.cloned.1.call-update
  9.1 0.0 reduce-scatter.11.cloned.1.call-start
  9.1 0.0 copy-done
  9.2 1.5 fusion.48
  10.7 0.1 copy_bitcast_fusion
  10.8 93.0 %all-gather.6.cloned.1.call-done = bf16[4096,1024]{1,0:T(8,128)(2,1)} async-done(((bf16[512,1024]{1,0:T(8,128)(2,1)}), bf16[4096,1024]{1,0:T(8,128)(2,1)}) %all-gather.6.cloned.1.call-update) | async-done | bytes 8388624 | tf_op jit(solution)/shard_map/all_gather | solution.py:23
  103.8 0.0 copy-done.1
  103.8 14.5 %convolution_bitcast_fusion = f32[4096,1024]{0,1:T(8,128)} fusion(bf16[4096,1024]{1,0:T(8,128)(2,1)} %all-gather.6.cloned.1.call-done, bf16[512,512]{1,0:T(8,128)(2,1)S(1)} %get-tuple-element.23, bf16[512,512]{1,0:T(8,128)(2,1)S(1)} %get-tuple-element.24, bf16[512,1024]{1,0:T(8,128)(2,1)S(1)} %bitcast.104), kind=kOutput, calls=%fused_computation | convolution fusion | flops 8596226048 | bytes 27262976 | tf_op jit(solution)/shard_map/dot_general | solution.py:25
  118.3 0.0 copy-start.2
  118.3 0.0 copy-start.3
  118.3 0.0 reduce-scatter.11.cloned.1.call-update
  118.3 0.0 reduce-scatter.13.cloned.1.call-start
  118.4 1.0 copy-done.2
  119.3 0.0 copy-start.4
  119.3 0.7 fusion.49
  120.1 0.5 copy.39
  120.6 0.5 copy.40
  121.0 0.0 copy-done.3
  121.1 14.9 %all-gather = f32[8,32,2]{1,2,0:T(2,128)S(1)} all-gather(f32[1,32,2]{1,2,0:T(2,128)S(1)} %bitcast.131), channel_id=1, replica_groups=mesh['row'=16,'col'=8,'chan'=2] {'col'}, dimensions={0}, use_global_device_ids=true | all-gather | bytes 2304 | tf_op jit(solution)/shard_map/all_gather | solution.py:47
  135.9 0.1 reshape.72
  136.0 98.7 %reduce-scatter.11.cloned.1.call-done = f32[256,1024]{0,1:T(8,128)} async-done(((f32[4096,1024]{0,1:T(8,128)}), f32[256,1024]{0,1:T(8,128)}) %reduce-scatter.11.cloned.1.call-update) | async-done | bytes 1048592 | tf_op jit(solution)/shard_map/reduce_scatter | solution.py:24
  234.7 1.4 compare_select_fusion.1
  236.1 1.7 convolution_bitcast_fusion.3
  237.8 0.0 reduce-scatter.13.cloned.1.call-update
  237.8 0.0 reduce-scatter.15.cloned.1.call-start
  237.9 0.7 fusion.28
  238.5 0.0 copy-done.4
  238.5 0.6 dynamic-slice
  239.8 38.1 %all-reduce = f32[512]{0:T(512)S(1)} all-reduce(f32[512]{0:T(512)S(1)} %bitcast.128), channel_id=4, replica_groups=mesh['row'=16,'col'=8,'chan'=2] {'row'}, use_global_device_ids=true, to_apply=%region_2.0.clone | all-reduce | flops 512 | bytes 4096
  277.9 0.1 dynamic-slice.1
  278.0 37.9 %reduce-scatter.13.cloned.1.call-done = f32[32,2]{1,0:T(8,128)} async-done(((f32[512,2]{1,0:T(8,128)}), f32[32,2]{1,0:T(8,128)}) %reduce-scatter.13.cloned.1.call-update) | async-done | bytes 272
  315.8 0.8 copy.32
  316.6 22.7 %all-gather.1 = f32[16,32,2]{1,2,0:T(2,128)S(1)} all-gather(f32[1,32,2]{1,2,0:T(2,128)S(1)} %divide_bitcast_fusion.1), channel_id=1, replica_groups=mesh['row'=16,'col'=8,'chan'=2] {'row'}, dimensions={0}, use_global_device_ids=true | all-gather | bytes 4352 | tf_op jit(solution)/shard_map/all_gather | solution.py:70
  339.4 0.1 reshape.74
  339.4 25.7 %all_gather.27 = f32[2,4096]{1,0:T(2,128)S(1)} all-gather(f32[2,512]{1,0:T(2,128)S(1)} %bitcast.105), channel_id=1, replica_groups=mesh['row'=16,'col'=8,'chan'=2] {'col'}, dimensions={1}, use_global_device_ids=true | all-gather | bytes 36864 | tf_op jit(solution)/shard_map/all_gather | solution.py:71
  365.2 0.1 fusion.51
  365.3 1.7 convolution_bitcast_fusion.2
  366.9 0.0 reduce-scatter.15.cloned.1.call-update
  367.0 0.0 reduce-scatter.17.cloned.1.call-start
  367.0 0.6 fusion.26
  367.6 38.1 %all-reduce.1 = f32[512]{0:T(512)S(1)} all-reduce(f32[512]{0:T(512)S(1)} %bitcast.130), channel_id=6, replica_groups=mesh['row'=16,'col'=8,'chan'=2] {'row'}, use_global_device_ids=true, to_apply=%region_4.0.clone | all-reduce | flops 512 | bytes 4096
  405.8 0.1 dynamic-slice.3
  405.9 37.0 %reduce-scatter.15.cloned.1.call-done = f32[32,2]{1,0:T(8,128)} async-done(((f32[512,2]{1,0:T(8,128)}), f32[32,2]{1,0:T(8,128)}) %reduce-scatter.15.cloned.1.call-update) | async-done | bytes 272
  442.9 0.8 copy.34
  443.7 0.1 multiply_bitcast_fusion
  443.8 22.7 %all-gather.2 = f32[16,32,2]{1,2,0:T(2,128)S(1)} all-gather(f32[1,32,2]{1,2,0:T(2,128)S(1)} %multiply_bitcast_fusion), channel_id=1, replica_groups=mesh['row'=16,'col'=8,'chan'=2] {'row'}, dimensions={0}, use_global_device_ids=true | all-gather | bytes 4352 | tf_op jit(solution)/shard_map/all_gather | solution.py:70
  466.5 0.1 reshape.76
  466.6 25.7 %all_gather.29 = f32[2,4096]{1,0:T(2,128)S(1)} all-gather(f32[2,512]{1,0:T(2,128)S(1)} %bitcast.106), channel_id=1, replica_groups=mesh['row'=16,'col'=8,'chan'=2] {'col'}, dimensions={1}, use_global_device_ids=true | all-gather | bytes 36864 | tf_op jit(solution)/shard_map/all_gather | solution.py:71
  492.3 0.1 fusion.50
  492.4 1.7 convolution_bitcast_fusion.1
  494.0 0.0 reduce-scatter.17.cloned.1.call-update
  494.1 0.6 fusion.24
  494.7 38.1 %all-reduce.2 = f32[512]{0:T(512)S(1)} all-reduce(f32[512]{0:T(512)S(1)} %bitcast.129), channel_id=8, replica_groups=mesh['row'=16,'col'=8,'chan'=2] {'row'}, use_global_device_ids=true, to_apply=%region_6.0.clone | all-reduce | flops 512 | bytes 4096
  532.8 0.1 dynamic-slice.5
  532.9 37.1 %reduce-scatter.17.cloned.1.call-done = f32[32,2]{1,0:T(8,128)} async-done(((f32[512,2]{1,0:T(8,128)}), f32[32,2]{1,0:T(8,128)}) %reduce-scatter.17.cloned.1.call-update) | async-done | bytes 272
  570.0 0.8 copy.36
  570.8 22.7 %all-gather.3 = f32[16,32,2]{1,2,0:T(2,128)S(1)} all-gather(f32[1,32,2]{1,2,0:T(2,128)S(1)} %divide_bitcast_fusion), channel_id=1, replica_groups=mesh['row'=16,'col'=8,'chan'=2] {'row'}, dimensions={0}, use_global_device_ids=true | all-gather | bytes 4352 | tf_op jit(solution)/shard_map/all_gather | solution.py:70
  593.5 0.1 reshape.78
  593.6 25.7 %all_gather.31 = f32[2,4096]{1,0:T(2,128)S(1)} all-gather(f32[2,512]{1,0:T(2,128)S(1)} %bitcast.107), channel_id=1, replica_groups=mesh['row'=16,'col'=8,'chan'=2] {'col'}, dimensions={1}, use_global_device_ids=true | all-gather | bytes 36864 | tf_op jit(solution)/shard_map/all_gather | solution.py:71
  619.3 0.6 constant_dynamic-slice_fusion.1
  (15 shorter events, 0.1 us)
Async XLA Ops:
  6.5 2.6 copy-start
  6.5 97.2 %all-gather.6.cloned.1.call-start = ((), (), s32[]{:S(2)}) async-start(), calls=%async_computation.4 | async-start | bytes 9437184 | tf_op jit(solution)/shard_map/all_gather | solution.py:23
  9.1 94.7 %copy-start.1 = (bf16[64,8,2,512]{3,1,2,0:T(8,128)(2,1)S(1)}, bf16[64,8,2,512]{3,1,2,0:T(8,128)(2,1)}, u32[]{:S(2)}) copy-start(bf16[64,8,2,512]{3,1,2,0:T(8,128)(2,1)} %copy.41) | copy-start | bytes 3145732
  9.1 225.6 %reduce-scatter.11.cloned.1.call-start = ((), (), s32[]{:S(2)}) async-start(), calls=%async_computation.5 | async-start | bytes 17825792 | tf_op jit(solution)/shard_map/reduce_scatter | solution.py:24
  118.3 1.0 copy-start.2
  118.3 2.7 copy-start.3
  118.3 197.5 %reduce-scatter.13.cloned.1.call-start = ((), (), s32[]{:S(2)}) async-start(), calls=%async_computation.6 | async-start | bytes 278528
  119.3 119.2 %copy-start.4 = (u32[256]{0:T(256)S(1)}, u32[256]{0:T(256)}, u32[]{:S(2)}) copy-start(u32[256]{0:T(256)} %constant.34) | copy-start | bytes 3076
  237.8 205.1 %reduce-scatter.15.cloned.1.call-start = ((), (), s32[]{:S(2)}) async-start(), calls=%async_computation.7 | async-start | bytes 278528
  367.0 203.0 %reduce-scatter.17.cloned.1.call-start = ((), (), s32[]{:S(2)}) async-start(), calls=%async_computation.8 | async-start | bytes 278528
Sparse Core Ops, SparseCore 0:
  9.2 94.5 all-gather.5
  118.4 116.2 reduce-scatter.10
  238.2 77.6 reduce-scatter.12
  367.1 75.7 reduce-scatter.14
  494.2 75.7 reduce-scatter.16
where the time goes:
time: 627 us; the launch traced here: 626 us
  waiting for transfers between devices  304 us (48%)
  blocking collectives  275 us (44%)
  matrix products  21.5 us (3%)
  between operations  13.9 us (2%)
  local copies, waits for them, and re-layouts  11 us (2%)
    unnamed x3, blocking collectives  114 us
    unnamed x8, waiting for transfers between devices  112 us
    reduce_scatter x1, waiting for transfers between devices, body(): lax.psum_scatter(lax.dot_general(all_antennas, right_side, contract_last,...  98.7 us
    all_gather x1, waiting for transfers between devices, body(): all_antennas = lax.all_gather(flattened, 'col', axis=0, tiled=True)  93 us
    all_gather x3, blocking collectives, body(): everything = lax.all_gather(gain_block, 'col', axis=1, tiled=True)  77.2 us
    all_gather x3, blocking collectives, body(): gain_block = lax.all_gather(updated, 'row', axis=1, tiled=True)  68.1 us
    all_gather x1, blocking collectives, body(): row_gains = lax.all_gather(initial_gains, 'col', axis=1, tiled=True)  14.9 us
    dot_general x1, matrix products, body(): lax.dot_general(all_antennas, right_side, contract_last, preferred_elemen...  14.5 us
  transfers between devices with their start and end apart: 5, of which 5 were waited for; matrix products, arithmetic and copies ran while one was open for 1% of the time, Pallas kernels for 0%

commit v1 on v0

--- a/solution.py
+++ b/solution.py
@@ -2,6 +2,7 @@
 import jax.numpy as jnp
 from jax import lax
 from jax.sharding import PartitionSpec as P
+from jax.lax import all_to_all, psum
 
 ITERS = 3
 
@@ -67,7 +68,10 @@
                 everything, (column_index * row_count + row_index) * share_size, share_size, 1
             )
             updated = 0.5 * (updated + previous)
-        gain_block = lax.all_gather(updated, "row", axis=1, tiled=True)
+        gain_block = jnp.concatenate(
+            all_to_all(jnp.stack([updated for _ in range(psum(1, "row"))], axis=0), "row", 0, 0),
+            axis=1,
+        )
         everything = lax.all_gather(gain_block, "col", axis=1, tiled=True)
         row_gains = lax.dynamic_slice_in_dim(everything, row_index * block_row, block_row, 1)
     return lax.dynamic_slice_in_dim(everything, own_start, share_size, 1)

time: 627 us -> 596 us (0.951)
  blocking collectives: 275 us -> 217 us
  waiting for transfers between devices: 304 us -> 319 us
  starting transfers between devices: 0.17 us -> 10.1 us
    all_gather x3 -> x0, blocking collectives: 68.1 us -> none  [body(): gain_block = lax.all_gather(updated, 'row', axis=1, tiled=True)]
    all_to_all x0 -> x2, waiting for transfers between devices: none -> 15.1 us  [body(): all_to_all(jnp.stack([updated for _ in range(psum(1, 'row'))], axis=0), '...]
    all_to_all x0 -> x1, blocking collectives: none -> 12.3 us  [body(): all_to_all(jnp.stack([updated for _ in range(psum(1, 'row'))], axis=0), '...]
    all_to_all x0 -> x2, starting transfers between devices: none -> 9.88 us  [body(): all_to_all(jnp.stack([updated for _ in range(psum(1, 'row'))], axis=0), '...]
  transfers between devices with their start and end apart: 5 -> 7, of which waited for: 5 -> 7; matrix products, arithmetic and copies ran while one was open for 1% -> 1% of each run, Pallas kernels for 0% -> 0%
where the time goes in v1:
time: 596 us; the launch traced here: 595 us
  waiting for transfers between devices  319 us (54%)
  blocking collectives  217 us (36%)
  matrix products  21.4 us (4%)
  between operations  13.9 us (2%)
  local copies, waits for them, and re-layouts  12.3 us (2%)
  starting transfers between devices  10.1 us (2%)
    unnamed x3, blocking collectives  113 us
    unnamed x8, waiting for transfers between devices  112 us
    reduce_scatter x1, waiting for transfers between devices, body(): lax.psum_scatter(lax.dot_general(all_antennas, right_side, contract_last,...  98.6 us
    all_gather x1, waiting for transfers between devices, body(): all_antennas = lax.all_gather(flattened, 'col', axis=0, tiled=True)  93 us
    all_gather x3, blocking collectives, body(): everything = lax.all_gather(gain_block, 'col', axis=1, tiled=True)  77.2 us
    all_to_all x2, waiting for transfers between devices, body(): all_to_all(jnp.stack([updated for _ in range(psum(1, 'row'))], axis=0), '...  15.1 us
    all_gather x1, blocking collectives, body(): row_gains = lax.all_gather(initial_gains, 'col', axis=1, tiled=True)  14.9 us
    dot_general x1, matrix products, body(): lax.dot_general(all_antennas, right_side, contract_last, preferred_elemen...  14.5 us
  transfers between devices with their start and end apart: 7, of which 7 were waited for; matrix products, arithmetic and copies ran while one was open for 1% of the time, Pallas kernels for 0%

profile of v1, /device:TPU:64, one launch (start us, length us, event | category | flops | bytes accessed | tf_op | source)
XLA Modules:
  0.0 595.3 jit_solution(14023769056051089342)
XLA Ops:
  6.5 0.0 copy-start
  6.5 0.0 all-gather.3.cloned.1.call-start
  6.5 2.5 copy.36
  9.1 0.0 all-gather.3.cloned.1.call-update
  9.1 0.0 reduce-scatter.11.cloned.1.call-start
  9.2 0.0 copy-done
  9.2 1.5 fusion.49
  10.7 0.1 copy_bitcast_fusion
  10.8 93.0 %all-gather.3.cloned.1.call-done = bf16[4096,1024]{1,0:T(8,128)(2,1)} async-done(((bf16[512,1024]{1,0:T(8,128)(2,1)}), bf16[4096,1024]{1,0:T(8,128)(2,1)}) %all-gather.3.cloned.1.call-update) | async-done | bytes 8388624 | tf_op jit(solution)/shard_map/all_gather | solution.py:24
  103.8 0.0 copy-done.1
  103.8 14.5 %convolution_bitcast_fusion = f32[4096,1024]{0,1:T(8,128)} fusion(bf16[4096,1024]{1,0:T(8,128)(2,1)} %all-gather.3.cloned.1.call-done, bf16[512,512]{1,0:T(8,128)(2,1)S(1)} %get-tuple-element.23, bf16[512,512]{1,0:T(8,128)(2,1)S(1)} %get-tuple-element.24, bf16[512,1024]{1,0:T(8,128)(2,1)S(1)} %bitcast.86), kind=kOutput, calls=%fused_computation | convolution fusion | flops 8596226048 | bytes 27262976 | tf_op jit(solution)/shard_map/dot_general | solution.py:26
  118.3 0.0 reduce-scatter.11.cloned.1.call-update
  118.3 0.0 reduce-scatter.13.cloned.1.call-start
  118.3 1.0 copy-done.2
  119.3 0.7 fusion.50
  120.0 0.5 copy.34
  120.5 0.5 copy.35
  121.0 0.0 copy-done.3
  121.0 14.9 %all-gather = f32[8,32,2]{1,2,0:T(2,128)S(1)} all-gather(f32[1,32,2]{1,2,0:T(2,128)S(1)} %bitcast.113), channel_id=1, replica_groups=mesh['row'=16,'col'=8,'chan'=2] {'col'}, dimensions={0}, use_global_device_ids=true | all-gather | bytes 2304 | tf_op jit(solution)/shard_map/all_gather | solution.py:48
  135.9 0.1 reshape.102
  136.0 98.6 %reduce-scatter.11.cloned.1.call-done = f32[256,1024]{0,1:T(8,128)} async-done(((f32[4096,1024]{0,1:T(8,128)}), f32[256,1024]{0,1:T(8,128)}) %reduce-scatter.11.cloned.1.call-update) | async-done | bytes 1048592 | tf_op jit(solution)/shard_map/reduce_scatter | solution.py:25
  234.6 1.4 compare_select_fusion.1
  236.0 1.7 convolution_bitcast_fusion.3
  237.7 0.0 reduce-scatter.13.cloned.1.call-update
  237.7 0.7 fusion.28
  238.4 0.0 copy-done.4
  238.4 0.6 dynamic-slice
  239.6 38.1 %all-reduce = f32[512]{0:T(512)S(1)} all-reduce(f32[512]{0:T(512)S(1)} %bitcast.110), channel_id=4, replica_groups=mesh['row'=16,'col'=8,'chan'=2] {'row'}, use_global_device_ids=true, to_apply=%region_2.0.clone | all-reduce | flops 512 | bytes 4096
  277.8 0.1 dynamic-slice.1
  277.9 38.0 %reduce-scatter.13.cloned.1.call-done = f32[32,2]{1,0:T(8,128)} async-done(((f32[512,2]{1,0:T(8,128)}), f32[32,2]{1,0:T(8,128)}) %reduce-scatter.13.cloned.1.call-update) | async-done | bytes 272
  315.8 0.8 copy.27
  316.6 0.6 stack.27
  317.2 4.9 all-to-all-start
  322.2 0.0 reduce-scatter.15.cloned.1.call-start
  322.2 7.5 %all-to-all-done = f32[16,2,32]{2,1,0:T(2,128)S(1)} async-done(((f32[16,2,32]{2,1,0:T(2,128)}), f32[16,2,32]{2,1,0:T(2,128)S(1)}, u32[]{:S(2)}, u32[]{:S(2)}) %all-to-all-start) | async-done | bytes 4128 | tf_op jit(solution)/shard_map/all_to_all | solution.py:72
  329.8 0.1 reshape.94
  329.9 25.7 %all_gather.17 = f32[2,4096]{1,0:T(2,128)S(1)} all-gather(f32[2,512]{1,0:T(2,128)S(1)} %reshape.94), channel_id=1, replica_groups=mesh['row'=16,'col'=8,'chan'=2] {'col'}, dimensions={1}, use_global_device_ids=true | all-gather | bytes 36864 | tf_op jit(solution)/shard_map/all_gather | solution.py:75
  355.6 0.1 fusion.52
  355.7 1.7 convolution_bitcast_fusion.2
  357.3 0.0 reduce-scatter.15.cloned.1.call-update
  357.4 0.0 reduce-scatter.17.cloned.1.call-start
  357.4 0.6 fusion.26
  358.1 37.3 %all-reduce.1 = f32[512]{0:T(512)S(1)} all-reduce(f32[512]{0:T(512)S(1)} %bitcast.112), channel_id=6, replica_groups=mesh['row'=16,'col'=8,'chan'=2] {'row'}, use_global_device_ids=true, to_apply=%region_4.0.clone | all-reduce | flops 512 | bytes 4096
  395.3 0.1 dynamic-slice.3
  395.4 37.1 %reduce-scatter.15.cloned.1.call-done = f32[32,2]{1,0:T(8,128)} async-done(((f32[512,2]{1,0:T(8,128)}), f32[32,2]{1,0:T(8,128)}) %reduce-scatter.15.cloned.1.call-update) | async-done | bytes 272
  432.5 0.8 copy.29
  433.3 0.1 fusion.39
  433.3 12.3 %all_to_all.15 = f32[16,2,32]{2,1,0:T(2,128)S(1)} all-to-all(f32[16,2,32]{2,1,0:T(2,128)S(1)} %stack.31), channel_id=1, replica_groups=mesh['row'=16,'col'=8,'chan'=2] {'row'}, dimensions={0} | all-to-all | bytes 8192 | tf_op jit(solution)/shard_map/all_to_all | solution.py:72
  445.7 0.1 reshape.96
  445.8 25.7 %all_gather.18 = f32[2,4096]{1,0:T(2,128)S(1)} all-gather(f32[2,512]{1,0:T(2,128)S(1)} %reshape.96), channel_id=1, replica_groups=mesh['row'=16,'col'=8,'chan'=2] {'col'}, dimensions={1}, use_global_device_ids=true | all-gather | bytes 36864 | tf_op jit(solution)/shard_map/all_gather | solution.py:75
  471.5 0.1 fusion.51
  471.6 1.7 convolution_bitcast_fusion.1
  473.2 0.0 reduce-scatter.17.cloned.1.call-update
  473.3 0.6 fusion.24
  473.9 37.3 %all-reduce.2 = f32[512]{0:T(512)S(1)} all-reduce(f32[512]{0:T(512)S(1)} %bitcast.111), channel_id=8, replica_groups=mesh['row'=16,'col'=8,'chan'=2] {'row'}, use_global_device_ids=true, to_apply=%region_6.0.clone | all-reduce | flops 512 | bytes 4096
  511.2 0.1 dynamic-slice.5
  511.2 37.1 %reduce-scatter.17.cloned.1.call-done = f32[32,2]{1,0:T(8,128)} async-done(((f32[512,2]{1,0:T(8,128)}), f32[32,2]{1,0:T(8,128)}) %reduce-scatter.17.cloned.1.call-update) | async-done | bytes 272
  548.4 0.8 copy.31
  549.2 0.6 stack.35
  549.8 4.9 all-to-all-start.2
  554.7 7.6 %all-to-all-done.2 = f32[16,2,32]{2,1,0:T(2,128)S(1)} async-done(((f32[16,2,32]{2,1,0:T(2,128)}), f32[16,2,32]{2,1,0:T(2,128)S(1)}, u32[]{:S(2)}, u32[]{:S(2)}) %all-to-all-start.2) | async-done | bytes 4128 | tf_op jit(solution)/shard_map/all_to_all | solution.py:72
  562.3 0.1 reshape.98
  562.4 25.7 %all_gather.19 = f32[2,4096]{1,0:T(2,128)S(1)} all-gather(f32[2,512]{1,0:T(2,128)S(1)} %reshape.98), channel_id=1, replica_groups=mesh['row'=16,'col'=8,'chan'=2] {'col'}, dimensions={1}, use_global_device_ids=true | all-gather | bytes 36864 | tf_op jit(solution)/shard_map/all_gather | solution.py:75
  588.1 0.6 constant_dynamic-slice_fusion.1
  (20 shorter events, 0.1 us)
Async XLA Ops:
  6.5 2.6 copy-start
  6.5 97.2 %all-gather.3.cloned.1.call-start = ((), (), s32[]{:S(2)}) async-start(), calls=%async_computation.7 | async-start | bytes 9437184 | tf_op jit(solution)/shard_map/all_gather | solution.py:24
  9.1 94.7 %copy-start.1 = (bf16[64,8,2,512]{3,1,2,0:T(8,128)(2,1)S(1)}, bf16[64,8,2,512]{3,1,2,0:T(8,128)(2,1)}, u32[]{:S(2)}) copy-start(bf16[64,8,2,512]{3,1,2,0:T(8,128)(2,1)} %copy.36) | copy-start | bytes 3145732
  9.1 225.5 %reduce-scatter.11.cloned.1.call-start = ((), (), s32[]{:S(2)}) async-start(), calls=%async_computation.8 | async-start | bytes 17825792 | tf_op jit(solution)/shard_map/reduce_scatter | solution.py:25
  118.2 1.0 copy-start.2
  118.3 2.7 copy-start.3
  118.3 197.5 %reduce-scatter.13.cloned.1.call-start = ((), (), s32[]{:S(2)}) async-start(), calls=%async_computation.9 | async-start | bytes 278528
  119.3 119.1 %copy-start.4 = (u32[256]{0:T(256)S(1)}, u32[256]{0:T(256)}, u32[]{:S(2)}) copy-start(u32[256]{0:T(256)} %constant.34) | copy-start | bytes 3076
  317.2 12.5 %all-to-all-start = ((f32[16,2,32]{2,1,0:T(2,128)}), f32[16,2,32]{2,1,0:T(2,128)S(1)}, u32[]{:S(2)}, u32[]{:S(2)}) async-start(f32[16,2,32]{2,1,0:T(2,128)} %stack.27), calls=%async_computation.1 | async-start | bytes 32768 | tf_op jit(solution)/shard_map/all_to_all | solution.py:72
  322.2 110.3 %reduce-scatter.15.cloned.1.call-start = ((), (), s32[]{:S(2)}) async-start(), calls=%async_computation.10 | async-start | bytes 278528
  357.4 191.0 %reduce-scatter.17.cloned.1.call-start = ((), (), s32[]{:S(2)}) async-start(), calls=%async_computation.11 | async-start | bytes 278528
  549.8 12.5 %all-to-all-start.2 = ((f32[16,2,32]{2,1,0:T(2,128)}), f32[16,2,32]{2,1,0:T(2,128)S(1)}, u32[]{:S(2)}, u32[]{:S(2)}) async-start(f32[16,2,32]{2,1,0:T(2,128)} %stack.35), calls=%async_computation.3 | async-start | bytes 32768 | tf_op jit(solution)/shard_map/all_to_all | solution.py:72
Sparse Core Ops, SparseCore 0:
  9.2 94.5 all-gather.2
  118.4 116.1 reduce-scatter.10
  238.1 77.6 reduce-scatter.12
  357.5 74.9 reduce-scatter.14
  473.4 74.9 reduce-scatter.16
